TPU v7x, 256 devices: a whole 4x4x8 slice. The times are simulated.
256 devices in a mesh: ops: 8 (over x, core), sec: 32 (over z, y).
Axes of the slice: x: 4, y: 4, z: 8, core: 2. Of those that a mesh axis runs over, the one named last changes fastest.
Arguments:
- wavefunction: float32 [256, 2, 128, 128], P('sec'), may hold values from -6 to 6
- left_blocks: float32 [64, 256, 128, 128], P('ops', 'sec'), may hold values from -0.5 to 0.5
- right_blocks: float32 [64, 256, 128, 128], P('ops', 'sec'), may hold values from -0.0625 to 0.0625
- target_owner: int32 [8, 32, 8, 8, 1], P('ops'), may hold values from 0 to 31; in each aligned block of 64 rows (0 to 63, 64 to 127, ..., all dimensions but the last counted through in order) at most 3 rows name the same one
- target_local: int32 [8, 32, 8, 8], P('ops'), may hold values from 0 to 7
Outputs:
- sigma: float32 [256, 2, 128, 128], P('sec', None, 'ops')
Inputs may be any that keep to these rules, and one draw needn't show every extreme that they name: `target_owner`: among the 64 pairs [o, d, :, :, 0] of one device, at most 3 name the same owner, and some device's pairs name one owner exactly 3 times.
All inputs are finite; a program needn't handle non-finite values.
Results may differ from a plain program's by a relative error of at most 0.00013.
Values sent between devices are 32-bit elements; how exact they have to be, the bound alone decides.
A program may use at most 192 MiB of HBM per device.

v0:
```python
import jax
import jax.numpy as jnp
from jax import lax
from jax.sharding import PartitionSpec as P

exact_mode = lax.Precision.HIGHEST


def shards(wavefunction, left_blocks, right_blocks, target_owner, target_local):
    sec_count = lax.axis_size("sec")
    term_local = left_blocks.shape[0]
    sector_local = left_blocks.shape[1]
    vectors = wavefunction.shape[1]
    states = wavefunction.shape[2]
    pair_count = term_local * sector_local
    capacity = (pair_count + sec_count - 1) // sec_count + 1
    slot_count = sec_count * capacity
    my_index = lax.axis_index("sec")
    owner_all = target_owner[0, :, :, :, 0].reshape(sec_count, pair_count)
    local_all = target_local[0].reshape(sec_count, pair_count)
    own_owner = lax.dynamic_index_in_dim(owner_all, my_index, 0, keepdims=False)
    peer_onehot = (own_owner[:, None] == jnp.arange(sec_count, dtype=jnp.int32)[None, :]).astype(
        jnp.int32
    )
    earlier = jnp.cumsum(peer_onehot, axis=0) - peer_onehot
    send_slot = own_owner * capacity + jnp.sum(earlier * peer_onehot, axis=1)
    is_mine = owner_all == my_index
    mine_count = is_mine.astype(jnp.int32)
    position = jnp.cumsum(mine_count, axis=1) - mine_count
    source_base = jnp.arange(sec_count, dtype=jnp.int32)[:, None] * capacity
    recv_slot = jnp.where(is_mine, source_base + position, slot_count)
    slot_sector = (
        jnp.zeros((slot_count,), jnp.int32)
        .at[recv_slot.reshape(-1)]
        .set(local_all.reshape(-1), mode="drop")
    )
    half_applied = jnp.einsum("jvbe,kjde->kjvbd", wavefunction, right_blocks, precision=exact_mode)
    contrib = jnp.einsum("kjab,kjvbd->kjvad", left_blocks, half_applied, precision=exact_mode)
    contrib = contrib.reshape(pair_count, vectors, states, states)
    routed = (
        jnp.zeros((slot_count, vectors, states, states), jnp.float32).at[send_slot].set(contrib)
    )
    arrived = lax.all_to_all(routed, "sec", split_axis=0, concat_axis=0, tiled=True)
    flat_rows = arrived.reshape(slot_count, vectors * states * states)
    selector = (slot_sector[None, :] == jnp.arange(sector_local, dtype=jnp.int32)[:, None]).astype(
        jnp.float32
    )
    partial_sum = jnp.dot(
        selector, flat_rows, precision=exact_mode, preferred_element_type=jnp.float32
    )
    partial_sum = partial_sum.reshape(sector_local, vectors, states, states)
    return lax.psum_scatter(partial_sum, "ops", scatter_dimension=2, tiled=True)


def solution(mesh):
    placed = (
        P("sec", None, None, None),
        P("ops", "sec", None, None),
        P("ops", "sec", None, None),
        P("ops", None, None, None, None),
        P("ops", None, None, None),
    )
    return jax.shard_map(
        shards, mesh=mesh, in_specs=placed, out_specs=P("sec", None, "ops", None), check_vma=False
    )
```

profile of v0, /device:TPU:5, one launch (start us, length us, event | category | flops | bytes accessed | tf_op | source)
XLA Modules:
  0.0 454.8 jit_solution(12595762003790021204)
XLA Ops:
  6.5 0.0 copy-start
  6.5 0.9 copy.17
  7.5 0.1 fusion.8
  7.5 0.1 reduce_window_sum.26
  7.6 0.2 select_reduce_fusion
  7.9 9.2 %fusion.5 = f32[8,8,128,2,128]{4,2,3,0,1:T(8,128)S(1)} fusion(f32[8,8,128,128]{3,2,1,0:T(8,128)} %param.7, f32[8,2,128,128]{3,2,1,0:T(8,128)S(1)} %copy-done), kind=kOutput, calls=%fused_computation.8 | convolution fusion | flops 3221225472 | bytes 13631488 | tf_op jit(solution)/shard_map/jvbe,kjde->kjvbd/dot_general | solution.py:37
  17.0 10.0 %fusion.2 = f32[8,8,2,128,128]{4,3,2,1,0:T(8,128)} fusion(f32[8,8,128,2,128]{4,2,3,0,1:T(8,128)S(1)} %fusion.5, f32[8,8,128,128]{3,2,1,0:T(8,128)S(1)} %copy-done.2), kind=kOutput, calls=%fused_computation.5 | convolution fusion | flops 3221225472 | bytes 20971520 | tf_op jit(solution)/shard_map/kjab,kjvbd->kjvad/dot_general | solution.py:38
  27.1 9.0 %copy.20 = f32[64,2,128,128]{3,2,1,0:T(8,128)} copy(f32[64,2,128,128]{2,3,1,0:T(8,128)} %bitcast.72) | data formatting | bytes 16777216 | tf_op jit(solution)/shard_map/reshape | solution.py:39
  36.1 6.1 %broadcast_in_dim.10 = f32[96,2,128,128]{3,2,1,0:T(8,128)} broadcast(f32[]{:T(128)} %constant.12.clone.1), dimensions={} | broadcast | bytes 12582916 | tf_op jit(solution)/shard_map/broadcast_in_dim | solution.py:41
  42.1 16.2 %scatter_fusion = f32[96,2,128,128]{3,2,1,0:T(8,128)} fusion(f32[96,2,128,128]{3,2,1,0:T(8,128)} %broadcast_in_dim.10, s32[64]{0:T(128)S(1)} %fusion.12, f32[64,2,128,128]{3,2,1,0:T(8,128)} %copy.20), kind=kCustom, calls=%fused_computation.1 | custom fusion | bytes 25166080 | tf_op jit(solution)/shard_map/scatter | solution.py:41
  58.3 11.4 %all-to-all-start = ((f32[96,2,128,128]{3,2,1,0:T(8,128)}), f32[96,2,128,128]{3,2,1,0:T(8,128)}, u32[]{:S(2)}, u32[]{:S(2)}) async-start(f32[96,2,128,128]{3,2,1,0:T(8,128)} %scatter_fusion), calls=%async_computation | async-start | bytes 25165824 | tf_op jit(solution)/shard_map/all_to_all | solution.py:43
  69.7 0.0 reduce-scatter.5.cloned.1.call-start
  69.8 0.1 add.58
  69.9 0.1 add.59
  70.0 0.2 reduce_window_sum.24
  70.2 0.1 reduce_window_sum.25
  70.3 0.1 copy.16
  70.5 0.1 eq.51
  70.6 0.0 copy-done.4
  70.6 0.1 copy.18
  70.7 0.1 reshape.101
  70.9 8.2 %scatter_custom_fusion = s32[96]{0:T(128)S(1)} fusion(s32[2048]{0:T(1024)S(1)} %bitcast.78, s32[2048]{0:T(1024)S(1)} %reshape.101, s32[]{:T(128)} %constant.8.clone.1), kind=kCustom, calls=%fused_computation.25 | custom fusion | bytes 388 | tf_op jit(solution)/shard_map/scatter | solution.py:35
  79.1 278.2 %all-to-all-done = f32[96,2,128,128]{3,2,1,0:T(8,128)} async-done(((f32[96,2,128,128]{3,2,1,0:T(8,128)}), f32[96,2,128,128]{3,2,1,0:T(8,128)}, u32[]{:S(2)}, u32[]{:S(2)}) %all-to-all-start) | async-done | bytes 12582944 | tf_op jit(solution)/shard_map/all_to_all | solution.py:43
  357.2 17.7 %copy.37 = f32[12,8,256,128]{3,1,2,0:T(8,128)} copy(f32[12,8,256,128]{3,2,1,0:T(8,128)} %bitcast.30) | data formatting | bytes 25165824
  375.0 11.3 %copy.30 = f32[12,8,256,128]{3,2,1,0:T(8,128)} copy(f32[12,8,256,128]{3,1,2,0:T(8,128)} %copy.37) | data formatting | bytes 25165824
  386.3 15.4 %fusion = f32[8,2,128,128]{3,0,2,1:T(8,128)S(1)} fusion(f32[2,128,128,96]{2,1,0,3:T(8,128)} %bitcast.71, s32[96]{0:T(128)S(1)} %scatter_custom_fusion), kind=kOutput, calls=%fused_computation.3 | convolution fusion | flops 301990656 | bytes 13631872 | tf_op jit(solution)/shard_map/dot_general | solution.py:48
  401.6 0.1 copy.26
  401.7 1.3 copy.38
  403.1 0.0 reduce-scatter.5.cloned.1.call-update
  403.1 43.2 %reduce-scatter.5.cloned.1.call-done = f32[16,2048]{1,0:T(8,128)} async-done(((f32[128,2048]{1,0:T(8,128)}), f32[16,2048]{1,0:T(8,128)}) %reduce-scatter.5.cloned.1.call-update) | async-done | bytes 131088
  446.3 0.9 copy.32
  447.2 0.7 copy.22
  (14 shorter events, 0.1 us)
Async XLA Ops:
  6.5 1.3 copy-start
  7.6 9.4 %copy-start.2 = (f32[8,8,128,128]{3,2,1,0:T(8,128)S(1)}, f32[8,8,128,128]{3,2,1,0:T(8,128)}, u32[]{:S(2)}) copy-start(f32[8,8,128,128]{3,2,1,0:T(8,128)} %param.6) | copy-start | bytes 12582916
  58.3 11.9 %copy-start.3 = (s32[1,32,8,8,1]{1,4,3,2,0:T(1,128)S(1)}, s32[1,32,8,8,1]{1,4,3,2,0:T(1,128)}, u32[]{:S(2)}) copy-start(s32[1,32,8,8,1]{1,4,3,2,0:T(1,128)} %param.8) | copy-start | bytes 24580
  58.3 12.2 %copy-start.4 = (s32[1,32,8,8]{1,3,2,0:T(8,128)S(1)}, s32[1,32,8,8]{1,3,2,0:T(8,128)}, u32[]{:S(2)}) copy-start(s32[1,32,8,8]{1,3,2,0:T(8,128)} %param.9) | copy-start | bytes 24580
  58.3 298.9 %all-to-all-start = ((f32[96,2,128,128]{3,2,1,0:T(8,128)}), f32[96,2,128,128]{3,2,1,0:T(8,128)}, u32[]{:S(2)}, u32[]{:S(2)}) async-start(f32[96,2,128,128]{3,2,1,0:T(8,128)} %scatter_fusion), calls=%async_computation | async-start | bytes 25165824 | tf_op jit(solution)/shard_map/all_to_all | solution.py:43
  69.7 376.5 %reduce-scatter.5.cloned.1.call-start = ((), (), s32[]{:S(2)}) async-start(), calls=%async_computation.2 | async-start | bytes 1179648
  386.3 61.6 %copy-start.1 = (f32[8,2,128,128]{3,2,1,0:T(8,128)S(1)}, f32[8,2,128,128]{3,2,1,0:T(8,128)}, u32[]{:S(2)}) copy-start(f32[8,2,128,128]{3,2,1,0:T(8,128)} %param.5) | copy-start | bytes 3145732
Sparse Core Ops, SparseCore 0:
  403.2 43.0 reduce-scatter.4
where the time goes:
time: 459 us; the launch traced here: 455 us
  waiting for transfers between devices  321 us (70%)
  local copies, waits for them, and re-layouts  73.2 us (16%)
  matrix products  34.6 us (8%)
  between operations  13.5 us (3%)
  starting transfers between devices  11.4 us (2%)
    all_to_all x1, waiting for transfers between devices, shards(): lax.all_to_all(routed, 'sec', split_axis=0, concat_axis=0, tiled=True)  278 us
    unnamed x2, waiting for transfers between devices  43.2 us
    unnamed x16, local copies, waits for them, and re-layouts  31.5 us
    scatter x1, local copies, waits for them, and re-layouts, shards(): jnp.zeros((slot_count, vectors, states, states), jnp.float32).at[send_slot]  16.2 us
    dot_general x1, matrix products, shards(): jnp.dot(selector, flat_rows, precision=exact_mode, preferred_element_type...  15.4 us
    all_to_all x1, starting transfers between devices, shards(): lax.all_to_all(routed, 'sec', split_axis=0, concat_axis=0, tiled=True)  11.4 us
    dot_general x1, matrix products, shards(): jnp.einsum('kjab,kjvbd->kjvad', left_blocks, half_applied, precision=exac...  10 us
  transfers between devices with their start and end apart: 2, of which 2 were waited for; matrix products, arithmetic and copies ran while one was open for 2% of the time, Pallas kernels for 0%

commit v1 on v0

v1 whole, which is shorter than its diff:
```python
import jax
import jax.numpy as jnp
from jax import lax
from jax.sharding import PartitionSpec as P


def shards(wavefunction, left_blocks, right_blocks, target_owner, target_local):
    sec_count = lax.axis_size("sec")
    ops_count = lax.axis_size("ops")
    term_local, sector_local, states = left_blocks.shape[:3]
    vectors = wavefunction.shape[1]
    pair_count = term_local * sector_local
    rows = states // ops_count
    me = lax.axis_index("sec")
    owner = lax.dynamic_index_in_dim(target_owner[0, :, :, :, 0], me, 0, keepdims=False)
    local = lax.dynamic_index_in_dim(target_local[0], me, 0, keepdims=False)
    target = (owner * sector_local + local).reshape(pair_count)
    targets = lax.all_gather(target, "ops", axis=0, tiled=True)
    high = lax.Precision.HIGH
    half = jnp.einsum("jvbe,kjde->kjvbd", wavefunction, right_blocks, precision=high)
    contrib = jnp.einsum("kjab,kjvbd->kjvad", left_blocks, half, precision=high)
    split = contrib.reshape(pair_count, vectors, ops_count, rows, states)
    split = split.transpose(2, 0, 1, 3, 4)
    arrived = lax.all_to_all(split, "ops", split_axis=0, concat_axis=0, tiled=True)
    flat = arrived.reshape(ops_count * pair_count, vectors * rows * states)
    total = sec_count * sector_local
    selector = (targets[None, :] == jnp.arange(total, dtype=jnp.int32)[:, None]).astype(jnp.float32)
    dense = jnp.dot(selector, flat, precision=high, preferred_element_type=jnp.float32)
    dense = dense.reshape(total, vectors, rows, states)
    return lax.psum_scatter(dense, "sec", scatter_dimension=0, tiled=True)


def solution(mesh):
    placed = (
        P("sec", None, None, None),
        P("ops", "sec", None, None),
        P("ops", "sec", None, None),
        P("ops", None, None, None, None),
        P("ops", None, None, None),
    )
    return jax.shard_map(
        shards, mesh=mesh, in_specs=placed, out_specs=P("sec", None, "ops", None), check_vma=False
    )
```

time: 459 us -> 390 us (0.85)
  waiting for transfers between devices: 321 us -> 219 us
  blocking collectives: 0 us -> 90.4 us
  local copies, waits for them, and re-layouts: 73.2 us -> 26.8 us
  matrix products: 34.6 us -> 24.8 us
    all_to_all x1, waiting for transfers between devices: 278 us -> 0.01 us  [shards(): lax.all_to_all(split, 'ops', split_axis=0, concat_axis=0, tiled=True)]
    reduce_scatter x0 -> x1, waiting for transfers between devices: none -> 219 us  [shards(): return lax.psum_scatter(dense, 'sec', scatter_dimension=0, tiled=True)]
    unnamed x0 -> x1, blocking collectives: none -> 90.4 us
    unnamed x2 -> x1, waiting for transfers between devices: 43.2 us -> 0.02 us
    unnamed x16 -> x12, local copies, waits for them, and re-layouts: 31.5 us -> 1.83 us
    scatter x2 -> x0, local copies, waits for them, and re-layouts: 24.4 us -> none  [the longest x1 16.2 us: shards(): jnp.zeros((slot_count, vectors, states, states), jnp.float32).at[send_slot]]
    dot_general x3, matrix products: 34.6 us -> 24.8 us  [the longest x1 10.5 us: shards(): jnp.dot(selector, flat, precision=high, preferred_element_type=jnp.float32)]
    dot_general x0 -> x1, local copies, waits for them, and re-layouts: none -> 9 us  [shards(): jnp.dot(selector, flat, precision=high, preferred_element_type=jnp.float32)]
  transfers between devices with their start and end apart: 2 -> 2, of which waited for: 2 -> 1; matrix products, arithmetic and copies ran while one was open for 2% -> 1% of each run, Pallas kernels for 0% -> 0%
where the time goes in v1:
time: 390 us; the launch traced here: 384 us
  waiting for transfers between devices  219 us (56%)
  blocking collectives  90.4 us (23%)
  local copies, waits for them, and re-layouts  26.8 us (7%)
  matrix products  24.8 us (6%)
  between operations  14.1 us (4%)
  starting transfers between devices  7.54 us (2%)
    reduce_scatter x1, waiting for transfers between devices, shards(): return lax.psum_scatter(dense, 'sec', scatter_dimension=0, tiled=True)  219 us
    unnamed x1, blocking collectives  90.4 us
    dot_general x1, matrix products, shards(): jnp.dot(selector, flat, precision=high, preferred_element_type=jnp.float32)  10.5 us
    reshape x1, local copies, waits for them, and re-layouts, shards(): flat = arrived.reshape(ops_count * pair_count, vectors * rows * states)  9.39 us
    dot_general x1, local copies, waits for them, and re-layouts, shards(): jnp.dot(selector, flat, precision=high, preferred_element_type=jnp.float32)  9 us
    dot_general x1, matrix products, shards(): jnp.einsum('jvbe,kjde->kjvbd', wavefunction, right_blocks, precision=high)  8.14 us
  transfers between devices with their start and end apart: 2, of which 1 were waited for; matrix products, arithmetic and copies ran while one was open for 1% of the time, Pallas kernels for 0%

profile of v1, /device:TPU:5, one launch (start us, length us, event | category | flops | bytes accessed | tf_op | source)
XLA Modules:
  0.0 384.3 jit_solution(11700039958910184261)
XLA Ops:
  6.5 0.0 copy-start
  6.5 0.0 copy-start.1
  6.5 1.2 copy-done
  7.8 8.1 %fusion.3 = f32[8,8,128,2,128]{2,4,3,0,1:T(8,128)} fusion(f32[8,8,128,128]{3,2,1,0:T(8,128)} %param.7, f32[8,2,128,128]{3,2,1,0:T(8,128)S(1)} %copy-done), kind=kOutput, calls=%fused_computation.4 | convolution fusion | flops 1610612736 | bytes 13631488 | tf_op jit(solution)/shard_map/jvbe,kjde->kjvbd/dot_general | solution.py:20
  15.9 0.0 copy-done.1
  15.9 6.1 %fusion = f32[8,8,2,128,128]{3,4,2,1,0:T(8,128)S(1)} fusion(f32[8,8,128,2,128]{2,4,3,0,1:T(8,128)} %fusion.3, f32[8,8,128,128]{3,2,1,0:T(8,128)S(1)} %copy-done.1), kind=kOutput, calls=%fused_computation | convolution fusion | flops 1610612736 | bytes 20971520 | tf_op jit(solution)/shard_map/kjab,kjvbd->kjvad/dot_general | solution.py:21
  22.0 4.5 %copy.14 = f32[64,2,8,16,128]{4,3,1,0,2:T(8,128)} copy(f32[64,2,8,16,128]{4,3,2,1,0:T(8,128)S(1)} %bitcast.35) | data formatting | bytes 16777216 | tf_op jit(solution)/shard_map/reshape | solution.py:22
  26.6 0.0 copy-start.2
  26.6 0.0 copy-start.3
  26.6 0.0 copy-start.4
  26.6 7.5 %all-to-all-start = ((f32[8,64,2,16,128]{4,3,2,1,0:T(8,128)}), f32[8,64,2,16,128]{4,3,2,1,0:T(8,128)}, u32[]{:S(2)}, u32[]{:S(2)}) async-start(f32[8,64,2,16,128]{4,3,2,1,0:T(8,128)} %bitcast.33), calls=%async_computation | async-start | bytes 16777216 | tf_op jit(solution)/shard_map/all_to_all | solution.py:24
  34.1 0.0 reduce-scatter.2.cloned.1.call-start
  34.1 0.0 copy-done.2
  34.1 1.3 multiply_reduce_fusion
  35.4 0.1 mul.12
  35.5 0.0 copy-done.3
  35.5 0.3 dynamic-slice_reduce_fusion
  35.8 0.1 squeeze.7
  35.9 0.0 copy-done.4
  35.9 0.6 dynamic-slice.2
  37.1 0.1 add_dynamic-update-slice_fusion
  37.2 90.4 %all-reduce = s32[512]{0:T(512)S(1)} all-reduce(s32[512]{0:T(512)S(1)} %add_dynamic-update-slice_fusion), channel_id=1, replica_groups=mesh['ops'=8,'sec'=32] {'ops'}, use_global_device_ids=true, to_apply=%add | all-reduce | flops 512 | bytes 4096
  127.6 0.0 all-to-all-done
  127.6 9.4 %reshape.19 = f32[512,4096]{1,0:T(8,128)} reshape(f32[8,64,2,16,128]{4,3,2,1,0:T(8,128)} %all-to-all-done) | data formatting | bytes 16777216 | tf_op jit(solution)/shard_map/reshape | solution.py:25
  137.0 9.0 %copy.8 = f32[4096,512]{1,0:T(8,128)} copy(f32[4096,512]{0,1:T(8,128)} %bitcast.36) | data formatting | bytes 16777216 | tf_op jit(solution)/shard_map/dot_general | solution.py:28
  146.0 10.5 %fusion.7 = f32[256,2,16,128]{3,0,2,1:T(8,128)} fusion(f32[2,16,128,512]{3,2,1,0:T(8,128)} %bitcast.34, s32[512]{0:T(512)S(1)} %all-reduce), kind=kOutput, calls=%fused_computation.9 | convolution fusion | flops 3221356544 | bytes 12584960 | tf_op jit(solution)/shard_map/dot_general | solution.py:28
  156.5 0.0 reduce-scatter.2.cloned.1.call-update
  156.6 219.3 %reduce-scatter.2.cloned.1.call-done = f32[8,2,16,128]{3,0,2,1:T(8,128)} async-done(((f32[256,2,16,128]{3,0,2,1:T(8,128)}), f32[8,2,16,128]{3,0,2,1:T(8,128)}) %reduce-scatter.2.cloned.1.call-update) | async-done | bytes 131088 | tf_op jit(solution)/shard_map/reduce_scatter | solution.py:30
  375.9 1.6 copy.9
  (1 shorter events, 0.0 us)
Async XLA Ops:
  6.5 1.2 copy-start
  6.5 9.4 %copy-start.1 = (f32[8,8,128,128]{3,2,1,0:T(8,128)S(1)}, f32[8,8,128,128]{3,2,1,0:T(8,128)}, u32[]{:S(2)}) copy-start(f32[8,8,128,128]{3,2,1,0:T(8,128)} %param.6) | copy-start | bytes 12582916
  26.6 7.6 %copy-start.2 = (s32[1,32,8,8,1]{1,4,3,2,0:T(1,128)S(1)}, s32[1,32,8,8,1]{1,4,3,2,0:T(1,128)}, u32[]{:S(2)}) copy-start(s32[1,32,8,8,1]{1,4,3,2,0:T(1,128)} %param.8) | copy-start | bytes 24580
  26.6 8.9 %copy-start.3 = (s32[1,32,8,8]{1,3,2,0:T(8,128)S(1)}, s32[1,32,8,8]{1,3,2,0:T(8,128)}, u32[]{:S(2)}) copy-start(s32[1,32,8,8]{1,3,2,0:T(8,128)} %param.9) | copy-start | bytes 24580
  26.6 9.3 %copy-start.4 = (u32[256]{0:T(256)S(1)}, u32[256]{0:T(256)}, u32[]{:S(2)}) copy-start(u32[256]{0:T(256)} %constant.23) | copy-start | bytes 3076
  26.6 101.1 %all-to-all-start = ((f32[8,64,2,16,128]{4,3,2,1,0:T(8,128)}), f32[8,64,2,16,128]{4,3,2,1,0:T(8,128)}, u32[]{:S(2)}, u32[]{:S(2)}) async-start(f32[8,64,2,16,128]{4,3,2,1,0:T(8,128)} %bitcast.33), calls=%async_computation | async-start | bytes 16777216 | tf_op jit(solution)/shard_map/all_to_all | solution.py:24
  34.1 341.8 %reduce-scatter.2.cloned.1.call-start = ((), (), s32[]{:S(2)}) async-start(), calls=%async_computation.2 | async-start | bytes 4325376 | tf_op jit(solution)/shard_map/reduce_scatter | solution.py:30
Sparse Core Ops, SparseCore 0:
  156.7 219.1 reduce-scatter.1

commit v2 on v1

v2 whole, which is shorter than its diff:
```python
import functools
import jax
import jax.numpy as jnp
from jax import lax
from jax.experimental import pallas as pl
from jax.experimental.pallas import tpu as pltpu
from jax.sharding import PartitionSpec as P

MESH = pl.DeviceIdType.MESH
F32, BF16 = jnp.float32, jnp.bfloat16
PAIRS, STATES, SECTORS, GROUPS = 64, 128, 8, 4
PER = PAIRS // GROUPS
TARGETS, NX, NY, NZ = 256, 4, 4, 8


def split(value):
    high = value.astype(BF16)
    return high, (value - high.astype(F32)).astype(BF16)


def dev(x, c, y, z):
    return (x * 2 + c, z * NY + y)


def kernel(tab_ref, psi_hbm, left_hbm, right_hbm, out_ref,
           psi, psic, left, right, send, recv, dense, recv2, send3, recv3, tabs, hot,
           in_sem, tab_s, tab_r, s1_s, s1_r, own_sem, s2_s, s2_r, s3_s, s3_r):
    o, s = lax.axis_index("ops"), lax.axis_index("sec")
    x, c, y, z = o // 2, o % 2, s % NY, s // NY
    own = (o, y * 2 + c)

    def row_peer(v, r):
        return dev(r // 2, r % 2, y, z) if v == 0 else dev(x, r % 2, r // 2, z)

    def dense_peer(v, b):
        return dev(x, c, b, z) if v == 0 else dev(b, c, y, z)

    def home_peer(v, b):
        return dev(x, c, y, b) if v == 0 else dev(y, c, x, b)

    psi_copy = pltpu.make_async_copy(psi_hbm, psi, in_sem.at[2, 0])
    psi_copy.start()

    def block_copies(g):
        rows = pl.ds(g * PER, PER)
        return (
            pltpu.make_async_copy(left_hbm.at[rows], left.at[rows], in_sem.at[0, g]),
            pltpu.make_async_copy(right_hbm.at[rows], right.at[rows], in_sem.at[1, g]),
        )

    for g in range(GROUPS):
        for copy in block_copies(g):
            copy.start()

    barrier = pltpu.get_barrier_semaphore()

    def greet(peer):
        pl.semaphore_signal(barrier, inc=1, device_id=peer, device_id_type=MESH)

    for d in range(1, 8):
        greet(row_peer(0, (own[0] + d) % 8))
        if d != 1:
            r = (own[1] // 2 + d // 2) % NY * 2 + (c + d) % 2
            greet(row_peer(1, r))
        greet(home_peer(0, (z + d) % NZ))

    @pl.when(x != y)
    def _():
        for d in range(NZ):
            greet(home_peer(1, (z + d) % NZ))

    pl.semaphore_wait(barrier, jnp.where(x == y, 20, 20 + NZ))

    def other(v, d):
        return (own[v] // 2 + d // 2) % 4 * 2 + (c + d) % 2

    def tab_copy(v, d):
        r = other(v, d)
        return pltpu.make_async_remote_copy(
            src_ref=tab_ref, dst_ref=tabs.at[v, own[v]],
            send_sem=tab_s.at[v, r], recv_sem=tab_r.at[v, own[v]],
            device_id=row_peer(v, r), device_id_type=MESH)

    def tab_wait(v, d):
        r = other(v, d)
        return pltpu.make_async_remote_copy(
            src_ref=tab_ref, dst_ref=tabs.at[v, r],
            send_sem=tab_s.at[v, r], recv_sem=tab_r.at[v, r],
            device_id=row_peer(v, r), device_id_type=MESH)

    def row_copy(v, h, d, rows):
        r = other(v, d)
        return pltpu.make_async_remote_copy(
            src_ref=send.at[v, h, r, rows], dst_ref=recv.at[v, h, own[v], rows],
            send_sem=s1_s.at[v, h, r], recv_sem=s1_r.at[v, h, own[v]],
            device_id=row_peer(v, r), device_id_type=MESH)

    def row_wait(v, h, d):
        r = other(v, d)
        return pltpu.make_async_remote_copy(
            src_ref=send.at[v, h, r], dst_ref=recv.at[v, h, r],
            send_sem=s1_s.at[v, h, r], recv_sem=s1_r.at[v, h, r],
            device_id=row_peer(v, r), device_id_type=MESH)

    for d in range(1, 8):
        for v in range(2):
            tab_copy(v, d).start()
    for v in range(2):
        tabs[v, own[v]] = tab_ref[...]

    psi_copy.wait()

    @pl.loop(0, SECTORS)
    def _(j):
        high, low = split(psi[j].reshape(2 * STATES, STATES))
        psic[j] = jnp.concatenate([high, high, low], axis=1)

    @pl.loop(0, GROUPS)
    def _(g):
        for copy in block_copies(g):
            copy.wait()

        @pl.loop(0, PER)
        def _(i):
            p = g * PER + i
            high, low = split(right[p])
            half = lax.dot_general(
                psic[p % SECTORS], jnp.concatenate([high, low, high], axis=1),
                (((1,), (1,)), ((), ())), preferred_element_type=F32)
            wide = jnp.concatenate([half[:STATES], half[STATES:]], axis=1)
            high, low = split(wide)
            operand = jnp.concatenate([high, low, high], axis=0)
            high, low = split(left[p])
            product = jnp.dot(
                jnp.concatenate([high, high, low], axis=1), operand, preferred_element_type=F32)
            for q in range(16):
                for v in range(2):
                    send[v, q % 2, q // 2, p] = product[8 * q:8 * q + 8, STATES * v:STATES * (v + 1)]

        for d in range(1, 8):
            for v in range(2):
                row_copy(v, 0, d, pl.ds(g * PER, PER)).start()

    for d in range(1, 8):
        for v in range(2):
            row_copy(v, 1, d, pl.ds(0, PAIRS)).start()

    def own_copy(v, h):
        return pltpu.make_async_copy(send.at[v, h, own[v]], recv.at[v, h, own[v]], own_sem.at[v, h])

    for h in range(2):
        for v in range(2):
            own_copy(v, h).start()

    for v in range(2):
        for d in range(1, 8):
            tab_wait(v, d).wait()
        for q in range(4):
            line = tabs[v, 2 * q][0:1, :] + tabs[v, 2 * q + 1][0:1, :]
            number = lax.broadcasted_iota(jnp.int32, (TARGETS, 128), 0)
            hot[v, :, 128 * q:128 * (q + 1)] = (number == line).astype(F32).astype(BF16)

    def dense_copy(v, h, d):
        b = ((y, x)[v] + d) % 4
        return pltpu.make_async_remote_copy(
            src_ref=dense.at[v, h, pl.ds(b * 512, 512)], dst_ref=recv2.at[v, h, d - 1],
            send_sem=s2_s.at[v, h, d - 1], recv_sem=s2_r.at[v, h, d - 1],
            device_id=dense_peer(v, b), device_id_type=MESH)

    def home_copy(v, h, d):
        b = (z + d) % NZ
        return pltpu.make_async_remote_copy(
            src_ref=send3.at[v, h, b], dst_ref=recv3.at[v, h, d],
            send_sem=s3_s.at[v, h, d], recv_sem=s3_r.at[v, h, d],
            device_id=home_peer(v, b), device_id_type=MESH)

    for h in range(2):
        for v in range(2):
            for d in range(1, 8):
                row_wait(v, h, d).wait_recv()
            own_copy(v, h).wait()
            flat = recv.at[v, h].reshape(8 * PAIRS * 8, 128)

            for i in range(8):
                high, low = split(flat[pl.ds(i, 512, stride=8), :])
                total = jnp.dot(hot[v], jnp.concatenate([high, low], axis=1), preferred_element_type=F32)
                dense[v, h, pl.ds(i, TARGETS, stride=8), :] = total[:, :128] + total[:, 128:]

            for d in range(1, 4):
                dense_copy(v, h, d).start()

        for v in range(2):
            for d in range(1, 4):
                dense_copy(v, h, d).wait_recv()
            mine = dense[v, h, pl.ds((y, x)[v] * 512, 512), :]
            total = mine + recv2[v, h, 0] + recv2[v, h, 1] + recv2[v, h, 2]
            send3[v, h] = total.reshape(NZ, SECTORS * 8, 128)
            for d in range(1, NZ):
                home_copy(v, h, d).start()
            if v == 0:
                recv3[v, h, 0] = send3[v, h, z]
            else:
                @pl.when(x == y)
                def _():
                    recv3[v, h, 0] = send3[v, h, z]

                @pl.when(x != y)
                def _():
                    home_copy(v, h, 0).start()

    for h in range(2):
        for v in range(2):
            for d in range(1, NZ):
                home_copy(v, h, d).wait_recv()
            if v == 1:
                @pl.when(x != y)
                def _():
                    home_copy(v, h, 0).wait_recv()
            total = recv3[v, h, 0]
            for d in range(1, NZ):
                total = total + recv3[v, h, d]
            out_ref[:, v, 8 * h:8 * h + 8, :] = total.reshape(SECTORS, 8, 128)

    for h in range(2):
        for v in range(2):
            for d in range(1, 8):
                row_wait(v, h, d).wait_send()
            for d in range(1, 4):
                dense_copy(v, h, d).wait_send()
            for d in range(1, NZ):
                home_copy(v, h, d).wait_send()

        @pl.when(x != y)
        def _():
            home_copy(1, h, 0).wait_send()


def shards(wavefunction, left_blocks, right_blocks, target_owner, target_local):
    o, s = lax.axis_index("ops"), lax.axis_index("sec")
    owner = lax.dynamic_index_in_dim(target_owner[0, :, :, :, 0], s, 0, keepdims=False)
    local = lax.dynamic_index_in_dim(target_local[0], s, 0, keepdims=False)
    line = (owner % NY * (NZ * SECTORS) + owner // NY * SECTORS + local).reshape(1, PAIRS)
    lanes = jnp.arange(128, dtype=jnp.int32)[None, :]
    table = jnp.where(lanes // PAIRS == o % 2, jnp.concatenate([line, line], axis=1), 0)
    table = jnp.broadcast_to(table, (8, 128))
    left = left_blocks.reshape(PAIRS, STATES, STATES)
    right = right_blocks.reshape(PAIRS, STATES, STATES)
    anywhere = pl.BlockSpec(memory_space=pl.ANY)
    near = pl.BlockSpec(memory_space=pltpu.VMEM)
    dma = pltpu.SemaphoreType.DMA
    return pl.pallas_call(
        kernel,
        out_shape=jax.ShapeDtypeStruct((SECTORS, 2, 16, STATES), F32),
        in_specs=[near, anywhere, anywhere, anywhere],
        out_specs=near,
        scratch_shapes=[
            pltpu.VMEM((SECTORS, 2, STATES, STATES), F32),
            pltpu.VMEM((SECTORS, 2 * STATES, 3 * STATES), BF16),
            pltpu.VMEM((PAIRS, STATES, STATES), F32),
            pltpu.VMEM((PAIRS, STATES, STATES), F32),
            pltpu.VMEM((2, 2, 8, PAIRS, 8, 128), F32),
            pltpu.VMEM((2, 2, 8, PAIRS, 8, 128), F32),
            pltpu.VMEM((2, 2, TARGETS * 8, 128), F32),
            pltpu.VMEM((2, 2, 3, 512, 128), F32),
            pltpu.VMEM((2, 2, NZ, SECTORS * 8, 128), F32),
            pltpu.VMEM((2, 2, NZ, SECTORS * 8, 128), F32),
            pltpu.VMEM((2, 8, 8, 128), jnp.int32),
            pltpu.VMEM((2, TARGETS, 512), BF16),
            dma((3, GROUPS)), dma((2, 8)), dma((2, 8)), dma((2, 2, 8)), dma((2, 2, 8)), dma((2, 2)),
            dma((2, 2, 3)), dma((2, 2, 3)), dma((2, 2, NZ)), dma((2, 2, NZ)),
        ],
        compiler_params=pltpu.CompilerParams(
            collective_id=0, has_side_effects=True, vmem_limit_bytes=52 << 20),
        name="sigma",
    )(table, wavefunction, left, right)


def solution(mesh):
    placed = (
        P("sec", None, None, None),
        P("ops", "sec", None, None),
        P("ops", "sec", None, None),
        P("ops", None, None, None, None),
        P("ops", None, None, None),
    )
    return jax.shard_map(
        shards, mesh=mesh, in_specs=placed, out_specs=P("sec", None, "ops", None), check_vma=False
    )
```

time: 390 us -> 134 us (0.34)
  the two profiles are of different devices: /device:TPU:5 before, /device:TPU:28 now
where the time goes in v2:
time: 134 us
  Pallas kernels  129 us (96%)
  local copies, waits for them, and re-layouts  5.15 us (4%)
    pallas_call x1, Pallas kernels, shards(): pl.pallas_call(kernel, out_shape=jax.ShapeDtypeStruct((SECTORS, 2, 16, ST...  129 us

profile of v2, /device:TPU:28, one launch (start us, length us, event | category | flops | bytes accessed | tf_op | source)
XLA Modules:
  0.0 134.1 jit_solution(6655597892460994065)
XLA Ops:
  0.0 0.0 copy-start
  0.0 0.8 copy-done
  0.8 1.3 dynamic-slice_reduce_fusion.1
  2.1 0.1 squeeze.9
  2.1 1.0 dynamic-slice_reduce_fusion
  3.2 0.1 squeeze.10
  3.3 0.1 compare_select_fusion
  3.4 0.0 copy-start.1
  3.4 1.2 copy-done.1
  4.6 128.9 %sigma.1 = f32[8,2,16,128]{3,2,1,0:T(8,128)S(1)} custom-call(s32[8,128]{1,0:T(8,128)S(1)} %broadcast_in_dim.4.tab_ref, f32[8,2,128,128]{3,2,1,0:T(8,128)S(1)} %copy-done.1, f32[64,128,128]{2,1,0:T(8,128)} %bitcast.2, f32[64,128,128]{2,1,0:T(8,128)} %bitcast.3), custom_call_target="tpu_custom_call" | custom-call | tf_op jit(solution)/shard_map/sigma/pallas_call | solution.py:251
  133.5 0.7 copy.7
  (2 shorter events, 0.0 us)
Async XLA Ops:
  0.0 0.8 copy-start
  3.4 1.2 copy-start.1

commit v3 on v1

v3 whole, which is shorter than its diff:
```python
import functools
import jax
import jax.numpy as jnp
from jax import lax
from jax.experimental import pallas as pl
from jax.experimental.pallas import tpu as pltpu
from jax.sharding import PartitionSpec as P

MESH = pl.DeviceIdType.MESH
F32, BF16 = jnp.float32, jnp.bfloat16
STATES, SECTORS, TERMS, PAIRS = 128, 8, 8, 64
GROUPS, PER, CHUNKS = 4, 2, 4
TARGETS, NX, NY, NZ = 256, 4, 4, 8


def split(value):
    high = value.astype(BF16)
    return high, (value - high.astype(F32)).astype(BF16)


def dev(x, c, y, z):
    return (x * 2 + c, z * NY + y)


def kernel(tab_ref, psi_hbm, left_hbm, right_hbm, out_ref,
           psi, left, right, send, recv, dense, recvz, sendy, recvy, recv2, sendz, recv3,
           sendt, recvt, tabs, hot,
           in_sem, tab_s, tab_r, s1_s, s1_r, own_sem, z_s, z_r, y_s, y_r,
           s2_s, s2_r, s3_s, s3_r, t_s, t_r):
    o, s = lax.axis_index("ops"), lax.axis_index("sec")
    x, c, y, z = o // 2, o % 2, s % NY, s // NY
    own = (o, y * 2 + c)
    side = (y, x)

    def row_peer(v, r):
        return dev(r // 2, r % 2, y, z) if v == 0 else dev(x, r % 2, r // 2, z)

    def side_peer(v, b):
        return dev(x, c, b, z) if v == 0 else dev(b, c, y, z)

    def far_peer(b):
        return dev(x, c, y, b)

    flipped = dev(y, c, x, z)

    psi_copy = pltpu.make_async_copy(psi_hbm, psi, in_sem.at[2, 0])
    psi_copy.start()

    def block_copies(j):
        return (
            pltpu.make_async_copy(left_hbm.at[:, j], left.at[j], in_sem.at[0, j]),
            pltpu.make_async_copy(right_hbm.at[:, j], right.at[j], in_sem.at[1, j]),
        )

    for j in range(SECTORS):
        for copy in block_copies(j):
            copy.start()

    barrier = pltpu.get_barrier_semaphore()

    def greet(peer):
        pl.semaphore_signal(barrier, inc=1, device_id=peer, device_id_type=MESH)

    def other(v, d):
        return (own[v] // 2 + d // 2) % 4 * 2 + (c + d) % 2

    for d in range(1, 8):
        greet(row_peer(0, other(0, d)))
        if d != 1:
            greet(row_peer(1, other(1, d)))
        greet(far_peer((z + d) % NZ))

    @pl.when(x != y)
    def _():
        greet(flipped)

    pl.semaphore_wait(barrier, jnp.where(x == y, 20, 21))

    def remote(src, dst, ssem, rsem, peer):
        return pltpu.make_async_remote_copy(
            src_ref=src, dst_ref=dst, send_sem=ssem, recv_sem=rsem,
            device_id=peer, device_id_type=MESH)

    def tab_copy(v, d, slot):
        r = other(v, d)
        return remote(tab_ref, tabs.at[v, slot], tab_s.at[v, r], tab_r.at[v, slot], row_peer(v, r))

    def row_copy(v, q, d, part):
        r = other(v, d)
        return remote(send.at[v, q, r, part], recv.at[v, q, own[v], part],
                      s1_s.at[v, q, r], s1_r.at[v, q, own[v]], row_peer(v, r))

    def row_wait(v, q, d):
        r = other(v, d)
        return remote(send.at[v, q, r], recv.at[v, q, r],
                      s1_s.at[v, q, r], s1_r.at[v, q, r], row_peer(v, r))

    def own_copy(v, q):
        return pltpu.make_async_copy(send.at[v, q, own[v]], recv.at[v, q, own[v]], own_sem.at[v, q])

    def z_copy(v, q, d):
        b = (z + d) % NZ
        return remote(dense.at[v, q, :, b], recvz.at[v, q, d],
                      z_s.at[v, q, d], z_r.at[v, q, d], far_peer(b))

    def y_copy(v, q, d):
        b = (side[v] + d) % 4
        return remote(sendy.at[v, q, b], recvy.at[v, q, d],
                      y_s.at[v, q, d], y_r.at[v, q, d], side_peer(v, b))

    def s2_copy(v, q, d):
        b = (side[v] + d) % 4
        return remote(dense.at[v, q, b], recv2.at[v, q - 2, d],
                      s2_s.at[v, q - 2, d], s2_r.at[v, q - 2, d], side_peer(v, b))

    def s3_copy(v, q, d):
        b = (z + d) % NZ
        return remote(sendz.at[v, q - 2, b], recv3.at[v, q - 2, d],
                      s3_s.at[v, q - 2, d], s3_r.at[v, q - 2, d], far_peer(b))

    def flip_copy(q):
        return remote(sendt.at[q], recvt.at[q], t_s.at[q], t_r.at[q], flipped)

    for d in range(1, 8):
        for v in range(2):
            tab_copy(v, d, own[v]).start()
    for v in range(2):
        tabs[v, own[v]] = tab_ref[...]

    psi_copy.wait()

    @pl.loop(0, GROUPS)
    def _(g):
        for i in range(PER):
            j = g * PER + i
            for copy in block_copies(j):
                copy.wait()
            high, low = split(psi[j].reshape(2 * STATES, STATES))
            vectors = jnp.concatenate([high, high, low], axis=1)
            high, low = split(right[j].reshape(TERMS * STATES, STATES))
            halves = lax.dot_general(
                jnp.concatenate([high, low, high], axis=1), vectors,
                (((1,), (1,)), ((), ())), preferred_element_type=F32)
            for k in range(TERMS):
                half = halves[STATES * k:STATES * (k + 1)]
                high, low = split(jnp.concatenate([half[:, :STATES], half[:, STATES:]], axis=0))
                operand = jnp.concatenate([high, low, high], axis=1)
                high, low = split(left[j, k])
                product = lax.dot_general(
                    jnp.concatenate([high, high, low], axis=1), operand,
                    (((1,), (1,)), ((), ())), preferred_element_type=F32)
                for t in range(32):
                    for v in range(2):
                        send[v, t % CHUNKS, t // CHUNKS, j, 4 * k:4 * k + 4, :] = product[
                            4 * t:4 * t + 4, STATES * v:STATES * (v + 1)]

        for d in range(1, 8):
            for v in range(2):
                row_copy(v, 0, d, pl.ds(g * PER, PER)).start()

    def start_rows(q):
        for d in range(1, 8):
            for v in range(2):
                row_copy(v, q, d, pl.ds(0, SECTORS)).start()

    start_rows(1)
    for q in range(CHUNKS):
        for v in range(2):
            own_copy(v, q).start()

    for v in range(2):
        for d in range(1, 8):
            tab_copy(v, d, other(v, d)).wait()
        for e in range(4):
            line = tabs[v, 2 * e][0:1, :] + tabs[v, 2 * e + 1][0:1, :]
            number = lax.broadcasted_iota(jnp.int32, (TARGETS, 128), 0)
            hot[v, :, 128 * e:128 * (e + 1)] = (number == line).astype(F32).astype(BF16)

    def sum_rows(q):
        for v in range(2):
            for d in range(1, 8):
                row_wait(v, q, d).wait_recv()
            own_copy(v, q).wait()
        if q + 2 < CHUNKS:
            start_rows(q + 2)
        for v in range(2):
            flat = recv.at[v, q].reshape(8 * PAIRS * 4, 128)
            sums = dense.at[v, q].reshape(TARGETS * 4, 128)
            for i in range(4):
                high, low = split(flat[pl.ds(i, 8 * PAIRS, stride=4), :])
                total = jnp.dot(hot[v], jnp.concatenate([high, low], axis=1), preferred_element_type=F32)
                sums[pl.ds(i, TARGETS, stride=4), :] = total[:, :128] + total[:, 128:]
            if q < 2:
                for d in range(1, NZ):
                    z_copy(v, q, d).start()
            else:
                for d in range(1, 4):
                    s2_copy(v, q, d).start()

    def finish(v, q, total):
        if v == 0:
            for n in range(SECTORS):
                out_ref[n, 0, 4 * q:4 * q + 4, :] = total[4 * n:4 * n + 4]
        else:
            sendt[q] = total

            @pl.when(x != y)
            def _():
                flip_copy(q).start()

            @pl.when(x == y)
            def _():
                recvt[q] = total

    def z_middle(q):
        for v in range(2):
            for d in range(1, NZ):
                z_copy(v, q, d).wait_recv()
            total = dense[v, q, :, z]
            for d in range(1, NZ):
                total = total + recvz[v, q, d]
            sendy[v, q] = total
            for d in range(1, 4):
                y_copy(v, q, d).start()

    def z_last(q):
        for v in range(2):
            for d in range(1, 4):
                y_copy(v, q, d).wait_recv()
            finish(v, q, sendy[v, q, side[v]] + recvy[v, q, 1] + recvy[v, q, 2] + recvy[v, q, 3])

    def s_middle(q):
        for v in range(2):
            for d in range(1, 4):
                s2_copy(v, q, d).wait_recv()
            sendz[v, q - 2] = (dense[v, q, side[v]] + recv2[v, q - 2, 1]) + (
                recv2[v, q - 2, 2] + recv2[v, q - 2, 3])
            for d in range(1, NZ):
                s3_copy(v, q, d).start()

    def s_last(q):
        for v in (1, 0):
            for d in range(1, NZ):
                s3_copy(v, q, d).wait_recv()
            total = sendz[v, q - 2, z]
            for d in range(1, NZ):
                total = total + recv3[v, q - 2, d]
            finish(v, q, total)

    sum_rows(0)
    sum_rows(1)
    sum_rows(2)
    z_middle(0)
    sum_rows(3)
    z_middle(1)
    s_middle(2)
    s_middle(3)
    z_last(0)
    z_last(1)
    s_last(2)
    s_last(3)

    for q in range(CHUNKS):
        @pl.when(x != y)
        def _():
            flip_copy(q).wait()

        for n in range(SECTORS):
            out_ref[n, 1, 4 * q:4 * q + 4, :] = recvt[q, 4 * n:4 * n + 4, :]

    for v in range(2):
        for q in range(CHUNKS):
            for d in range(1, 8):
                row_wait(v, q, d).wait_send()
        for q in range(2):
            for d in range(1, NZ):
                z_copy(v, q, d).wait_send()
                s3_copy(v, q + 2, d).wait_send()
            for d in range(1, 4):
                y_copy(v, q, d).wait_send()
                s2_copy(v, q + 2, d).wait_send()


def shards(wavefunction, left_blocks, right_blocks, target_owner, target_local):
    o, s = lax.axis_index("ops"), lax.axis_index("sec")
    owner = lax.dynamic_index_in_dim(target_owner[0, :, :, :, 0], s, 0, keepdims=False)
    local = lax.dynamic_index_in_dim(target_local[0], s, 0, keepdims=False)
    number = owner % NY * (NZ * SECTORS) + owner // NY * SECTORS + local
    line = number.T.reshape(1, PAIRS)
    lanes = jnp.arange(128, dtype=jnp.int32)[None, :]
    table = jnp.where(lanes // PAIRS == o % 2, jnp.concatenate([line, line], axis=1), 0)
    table = jnp.broadcast_to(table, (8, 128))
    far = pl.BlockSpec(memory_space=pltpu.HBM)
    near = pl.BlockSpec(memory_space=pltpu.VMEM)
    dma = pltpu.SemaphoreType.DMA

    def vmem(*shape):
        return pltpu.VMEM(shape, F32)

    return pl.pallas_call(
        kernel,
        out_shape=jax.ShapeDtypeStruct((SECTORS, 2, 16, STATES), F32),
        in_specs=[near, far, far, far],
        out_specs=near,
        scratch_shapes=[
            vmem(SECTORS, 2, STATES, STATES),
            vmem(SECTORS, TERMS, STATES, STATES),
            vmem(SECTORS, TERMS, STATES, STATES),
            vmem(2, CHUNKS, 8, SECTORS, 4 * TERMS, 128),
            vmem(2, CHUNKS, 8, SECTORS, 4 * TERMS, 128),
            vmem(2, CHUNKS, 4, NZ, 4 * SECTORS, 128),
            vmem(2, 2, NZ, 4, 4 * SECTORS, 128),
            vmem(2, 2, 4, 4 * SECTORS, 128),
            vmem(2, 2, 4, 4 * SECTORS, 128),
            vmem(2, 2, 4, NZ, 4 * SECTORS, 128),
            vmem(2, 2, NZ, 4 * SECTORS, 128),
            vmem(2, 2, NZ, 4 * SECTORS, 128),
            vmem(CHUNKS, 4 * SECTORS, 128),
            vmem(CHUNKS, 4 * SECTORS, 128),
            pltpu.VMEM((2, 8, 8, 128), jnp.int32),
            pltpu.VMEM((2, TARGETS, 512), BF16),
            dma((3, SECTORS)), dma((2, 8)), dma((2, 8)),
            dma((2, CHUNKS, 8)), dma((2, CHUNKS, 8)), dma((2, CHUNKS)),
            dma((2, 2, NZ)), dma((2, 2, NZ)), dma((2, 2, 4)), dma((2, 2, 4)),
            dma((2, 2, 4)), dma((2, 2, 4)), dma((2, 2, NZ)), dma((2, 2, NZ)),
            dma((CHUNKS,)), dma((CHUNKS,)),
        ],
        compiler_params=pltpu.CompilerParams(
            collective_id=0, has_side_effects=True, vmem_limit_bytes=52 << 20),
        name="sigma",
    )(table, wavefunction, left_blocks, right_blocks)


def solution(mesh):
    placed = (
        P("sec", None, None, None),
        P("ops", "sec", None, None),
        P("ops", "sec", None, None),
        P("ops", None, None, None, None),
        P("ops", None, None, None),
    )
    return jax.shard_map(
        shards, mesh=mesh, in_specs=placed, out_specs=P("sec", None, "ops", None), check_vma=False
    )
```

time: 390 us -> 101 us (0.26)
  waiting for transfers between devices: 219 us -> 0 us
  Pallas kernels: 0 us -> 94.9 us
  blocking collectives: 90.4 us -> 0 us
  matrix products: 24.8 us -> 0 us
  local copies, waits for them, and re-layouts: 26.8 us -> 4.01 us
  between operations: 14.1 us -> 0.03 us
  starting transfers between devices: 7.54 us -> 0 us
    reduce_scatter x1 -> x0, waiting for transfers between devices: 219 us -> none  [shards(): return lax.psum_scatter(dense, 'sec', scatter_dimension=0, tiled=True)]
    pallas_call x0 -> x1, Pallas kernels: none -> 94.9 us  [shards(): pl.pallas_call(kernel, out_shape=jax.ShapeDtypeStruct((SECTORS, 2, 16, ST...]
    unnamed x1 -> x0, blocking collectives: 90.4 us -> none
    dot_general x3 -> x0, matrix products: 24.8 us -> none  [the longest x1 10.5 us: shards(): jnp.dot(selector, flat, precision=high, preferred_element_type=jnp.float32)]
    reshape x2 -> x0, local copies, waits for them, and re-layouts: 13.9 us -> none  [the longest x1 9.39 us: shards(): flat = arrived.reshape(ops_count * pair_count, vectors * rows * states)]
    dot_general x1 -> x0, local copies, waits for them, and re-layouts: 9 us -> none  [shards(): jnp.dot(selector, flat, precision=high, preferred_element_type=jnp.float32)]
    all_to_all x1 -> x0, starting transfers between devices: 7.54 us -> none  [shards(): lax.all_to_all(split, 'ops', split_axis=0, concat_axis=0, tiled=True)]
  transfers between devices with their start and end apart: 2 -> 0, of which waited for: 1 -> 0; matrix products, arithmetic and copies ran while one was open for 1% -> 0% of each run, Pallas kernels for 0% -> 0%
where the time goes in v3:
time: 101 us; the launch traced here: 99 us
  Pallas kernels  94.9 us (94%)
  local copies, waits for them, and re-layouts  4.01 us (4%)
    pallas_call x1, Pallas kernels, shards(): pl.pallas_call(kernel, out_shape=jax.ShapeDtypeStruct((SECTORS, 2, 16, ST...  94.9 us
    unnamed x7, local copies, waits for them, and re-layouts  2.88 us

profile of v3, /device:TPU:5, one launch (start us, length us, event | category | flops | bytes accessed | tf_op | source)
XLA Modules:
  0.0 99.0 jit_solution(11480824564186546104)
XLA Ops:
  0.0 0.0 copy-start
  0.0 0.8 copy-done
  0.8 0.1 constant_dynamic-slice_fusion.1
  0.9 0.1 copy.9
  1.0 0.8 constant_dynamic-slice_fusion
  1.9 0.1 copy.10
  2.0 0.1 copy.8
  2.1 0.1 concatenate.10
  2.1 0.1 compare_select_fusion
  2.2 0.0 copy-start.1
  2.2 1.2 %copy-done.1 = f32[8,2,128,128]{3,2,1,0:T(8,128)S(1)} copy-done((f32[8,2,128,128]{3,2,1,0:T(8,128)S(1)}, f32[8,2,128,128]{3,2,1,0:T(8,128)}, u32[]{:S(2)}) %copy-start.1) | copy-done | bytes 1048600
  3.5 94.9 %sigma.1 = f32[8,2,16,128]{3,2,1,0:T(8,128)S(1)} custom-call(s32[8,128]{1,0:T(8,128)S(1)} %broadcast_in_dim.4.tab_ref, f32[8,2,128,128]{3,2,1,0:T(8,128)S(1)} %copy-done.1, f32[8,8,128,128]{3,2,1,0:T(8,128)} %left_hbm.1, f32[8,8,128,128]{3,2,1,0:T(8,128)} %right_hbm.1), custom_call_target="tpu_custom_call" | custom-call | tf_op jit(solution)/shard_map/sigma/pallas_call | solution.py:300
  98.4 0.7 copy.12
  (2 shorter events, 0.0 us)
Async XLA Ops:
  0.0 0.8 copy-start
  2.2 1.2 %copy-start.1 = (f32[8,2,128,128]{3,2,1,0:T(8,128)S(1)}, f32[8,2,128,128]{3,2,1,0:T(8,128)}, u32[]{:S(2)}) copy-start(f32[8,2,128,128]{3,2,1,0:T(8,128)} %psi_hbm.1) | copy-start | bytes 3145732

commit v4 on v3

v4 whole, which is shorter than its diff:
```python
import functools
import jax
import jax.numpy as jnp
from jax import lax
from jax.experimental import pallas as pl
from jax.experimental.pallas import tpu as pltpu
from jax.sharding import PartitionSpec as P

MESH = pl.DeviceIdType.MESH
F32, BF16 = jnp.float32, jnp.bfloat16
STATES, SECTORS, TERMS, PAIRS = 128, 8, 8, 64
GROUPS, PER, CHUNKS = 4, 2, 4
ROWS, FIRST = (6, 6, 2, 2), (0, 8, 6, 14)
TARGETS, NX, NY, NZ = 256, 4, 4, 8


def split(value):
    high = value.astype(BF16)
    return high, (value - high.astype(F32)).astype(BF16)


def dev(x, c, y, z):
    return (x * 2 + c, z * NY + y)


def kernel(tab_ref, psi_hbm, left_hbm, right_hbm, out_ref, *scratch):
    parts = iter(scratch)

    def take(count):
        return [next(parts) for _ in range(count)]

    psi, left, right, tabs, hot = take(5)
    send, recv, dense = take(CHUNKS), take(CHUNKS), take(CHUNKS)
    chain = take(2)
    sendy, recvy = take(2), take(2)
    recv2, sendz, recv3 = take(2), take(2), take(2)
    (in_sem, tab_s, tab_r, s1_s, s1_r, own_sem, l_s, l_r,
     y_s, y_r, s2_s, s2_r, s3_s, s3_r) = take(14)
    o, s = lax.axis_index("ops"), lax.axis_index("sec")
    x, c, y, z = o // 2, o % 2, s % NY, s // NY
    own = (o, y * 2 + c)
    side = (y, x)

    def row_peer(v, r):
        return dev(r // 2, r % 2, y, z) if v == 0 else dev(x, r % 2, r // 2, z)

    def side_peer(v, b):
        return dev(x, c, b, z) if v == 0 else dev(b, c, y, z)

    def home_peer(v, b):
        return dev(x, c, y, b) if v == 0 else dev(y, c, x, b)

    psi_copy = pltpu.make_async_copy(psi_hbm, psi, in_sem.at[2, 0])
    psi_copy.start()

    def block_copies(j):
        return (
            pltpu.make_async_copy(left_hbm.at[:, j], left.at[j], in_sem.at[0, j]),
            pltpu.make_async_copy(right_hbm.at[:, j], right.at[j], in_sem.at[1, j]),
        )

    for j in range(SECTORS):
        for copy in block_copies(j):
            copy.start()

    barrier = pltpu.get_barrier_semaphore()

    def greet(peer):
        pl.semaphore_signal(barrier, inc=1, device_id=peer, device_id_type=MESH)

    def other(v, d):
        return (own[v] // 2 + d // 2) % 4 * 2 + (c + d) % 2

    for d in range(1, 8):
        greet(row_peer(0, other(0, d)))
        if d != 1:
            greet(row_peer(1, other(1, d)))
        greet(home_peer(0, (z + d) % NZ))
    for d in range(1, 4):
        greet(dev((y + d) % 4, c, x, z))

    @pl.when(x != y)
    def _():
        greet(dev(y, c, x, z))
        for d in range(NZ):
            greet(home_peer(1, (z + d) % NZ))

    def remote(src, dst, ssem, rsem, peer):
        return pltpu.make_async_remote_copy(
            src_ref=src, dst_ref=dst, send_sem=ssem, recv_sem=rsem,
            device_id=peer, device_id_type=MESH)

    def tab_copy(v, d, slot):
        r = other(v, d)
        return remote(tab_ref, tabs.at[v, slot], tab_s.at[v, r], tab_r.at[v, slot], row_peer(v, r))

    def row_copy(v, q, d, part):
        r = other(v, d)
        return remote(send[q].at[v, r, part], recv[q].at[v, own[v], part],
                      s1_s.at[v, q, r], s1_r.at[v, q, own[v]], row_peer(v, r))

    def row_wait(v, q, d):
        r = other(v, d)
        return remote(send[q].at[v, r], recv[q].at[v, r],
                      s1_s.at[v, q, r], s1_r.at[v, q, r], row_peer(v, r))

    def own_copy(v, q):
        return pltpu.make_async_copy(send[q].at[v, own[v]], recv[q].at[v, own[v]], own_sem.at[v, q])

    def hops(v, way):
        return 4 if v == way else 3

    def link_copy(v, q, way, k):
        b = (z + 1 - 2 * way) % NZ
        far = (z + (1 - 2 * way) * hops(v, way)) % NZ
        source = dense[q].at[v, :, far] if k == 1 else chain[q].at[v, way, k - 2]
        return remote(source, chain[q].at[v, way, k - 1],
                      l_s.at[q, v, way, k - 1], l_r.at[q, v, way, k - 1], home_peer(0, b))

    def link(q, k):
        for v in range(2):
            for way in range(2):
                if k > hops(v, way):
                    continue
                if k > 1:
                    link_copy(v, q, way, k - 1).wait_recv()
                    b = (z + (1 - 2 * way) * (hops(v, way) - k + 1)) % NZ
                    chain[q][v, way, k - 2] = chain[q][v, way, k - 2] + dense[q][v, :, b]
                link_copy(v, q, way, k).start()

    def y_copy(v, q, d):
        b = (side[0] + d) % 4
        if v == 0:
            return remote(sendy[q].at[0, b], recvy[q].at[0, d],
                          y_s.at[q, 0, d], y_r.at[q, 0, d], dev(x, c, b, z))
        return remote(sendy[q].at[1, b], recvy[q].at[1, x],
                      y_s.at[q, 1, d], y_r.at[q, 1, x], dev(y, c, b, z))

    def y_wait(v, q, d):
        if v == 0:
            return y_copy(v, q, d)
        a = (y + d) % 4
        return remote(sendy[q].at[1, a], recvy[q].at[1, a],
                      y_s.at[q, 1, d], y_r.at[q, 1, a], dev(a, c, x, z))

    def s2_copy(v, q, d):
        b = (side[v] + d) % 4
        return remote(dense[q].at[v, b], recv2[q - 2].at[v, d],
                      s2_s.at[q - 2, v, d], s2_r.at[q - 2, v, d], side_peer(v, b))

    def s3_copy(v, q, d):
        b = (z + d) % NZ
        return remote(sendz[q - 2].at[v, b], recv3[q - 2].at[v, d],
                      s3_s.at[q - 2, v, d], s3_r.at[q - 2, v, d], home_peer(v, b))

    def compute(g):
        for i in range(PER):
            j = g * PER + i
            for copy in block_copies(j):
                copy.wait()
            high, low = split(psi[j].reshape(2 * STATES, STATES))
            vectors = jnp.concatenate([high, high, low], axis=1)
            high, low = split(right[j].reshape(TERMS * STATES, STATES))
            halves = lax.dot_general(
                jnp.concatenate([high, low, high], axis=1), vectors,
                (((1,), (1,)), ((), ())), preferred_element_type=F32)
            for k in range(TERMS):
                half = halves[STATES * k:STATES * (k + 1)]
                high, low = split(jnp.concatenate([half[:, :STATES], half[:, STATES:]], axis=0))
                operand = jnp.concatenate([high, low, high], axis=1)
                high, low = split(left[j, k])
                product = lax.dot_general(
                    jnp.concatenate([high, high, low], axis=1), operand,
                    (((1,), (1,)), ((), ())), preferred_element_type=F32)
                for r in range(8):
                    for q in range(CHUNKS):
                        n = ROWS[q]
                        first = 16 * r + FIRST[q]
                        for v in range(2):
                            send[q][v, r, j, n * k:n * k + n, :] = product[
                                first:first + n, STATES * v:STATES * (v + 1)]

    def start_group(g):
        for d in range(1, 8):
            for v in range(2):
                row_copy(v, 0, d, pl.ds(g * PER, PER)).start()

    psi_copy.wait()
    compute(0)
    pl.semaphore_wait(barrier, jnp.where(x == y, 23, 32))
    start_group(0)
    for d in range(1, 8):
        for v in range(2):
            tab_copy(v, d, own[v]).start()
    for v in range(2):
        tabs[v, own[v]] = tab_ref[...]

    @pl.loop(1, GROUPS)
    def _(g):
        compute(g)
        start_group(g)

    def start_rows(q):
        for d in range(1, 8):
            for v in range(2):
                row_copy(v, q, d, pl.ds(0, SECTORS)).start()

    start_rows(1)
    for q in range(CHUNKS):
        for v in range(2):
            own_copy(v, q).start()

    for v in range(2):
        for d in range(1, 8):
            tab_copy(v, d, other(v, d)).wait()
        for e in range(4):
            line = tabs[v, 2 * e][0:1, :] + tabs[v, 2 * e + 1][0:1, :]
            number = lax.broadcasted_iota(jnp.int32, (TARGETS, 128), 0)
            hot[v, :, 128 * e:128 * (e + 1)] = (number == line).astype(F32).astype(BF16)

    def sum_rows(q):
        n = ROWS[q]
        for v in range(2):
            for d in range(1, 8):
                row_wait(v, q, d).wait_recv()
            own_copy(v, q).wait()
        if q + 2 < CHUNKS:
            start_rows(q + 2)
        for v in range(2):
            flat = recv[q].at[v].reshape(8 * PAIRS * n, 128)
            sums = dense[q].at[v].reshape(TARGETS * n, 128)
            for i in range(n):
                high, low = split(flat[pl.ds(i, 8 * PAIRS, stride=n), :])
                total = jnp.dot(hot[v], jnp.concatenate([high, low], axis=1), preferred_element_type=F32)
                sums[pl.ds(i, TARGETS, stride=n), :] = total[:, :128] + total[:, 128:]
            if q >= 2:
                for d in range(1, 4):
                    s2_copy(v, q, d).start()
        if q < 2:
            link(q, 1)

    def finish(v, q, total):
        n = ROWS[q]
        for i in range(SECTORS):
            out_ref[i, v, FIRST[q]:FIRST[q] + n, :] = total[n * i:n * i + n]

    def start_y(v, q):
        for d in range(1, 4):
            y_copy(v, q, d).start()
        if v == 1:
            @pl.when(x != y)
            def _():
                y_copy(1, q, 0).start()

            @pl.when(x == y)
            def _():
                recvy[q][1, x] = sendy[q][1, x]

    def middle(q):
        for v in (1, 0):
            for way in range(2):
                link_copy(v, q, way, hops(v, way)).wait_recv()
            sendy[q][v] = dense[q][v, :, z] + (
                chain[q][v, 0, hops(v, 0) - 1] + chain[q][v, 1, hops(v, 1) - 1])
            start_y(v, q)

    def last_y(q):
        for v in range(2):
            for d in range(1, 4):
                y_wait(v, q, d).wait_recv()
            if v == 1:
                @pl.when(x != y)
                def _():
                    y_wait(1, q, 0).wait_recv()
            first = sendy[q][0, y] if v == 0 else recvy[q][1, 0]
            finish(v, q, (first + recvy[q][v, 1]) + (recvy[q][v, 2] + recvy[q][v, 3]))

    def s_middle(q):
        for v in (1, 0):
            for d in range(1, 4):
                s2_copy(v, q, d).wait_recv()
            sendz[q - 2][v] = (dense[q][v, side[v]] + recv2[q - 2][v, 1]) + (
                recv2[q - 2][v, 2] + recv2[q - 2][v, 3])
            for d in range(1, NZ):
                s3_copy(v, q, d).start()
            if v == 1:
                @pl.when(x != y)
                def _():
                    s3_copy(1, q, 0).start()

                @pl.when(x == y)
                def _():
                    recv3[q - 2][1, 0] = sendz[q - 2][1, z]

    def s_last(q):
        for v in range(2):
            for d in range(1, NZ):
                s3_copy(v, q, d).wait_recv()
            if v == 1:
                @pl.when(x != y)
                def _():
                    s3_copy(1, q, 0).wait_recv()
            total = sendz[q - 2][0, z] if v == 0 else recv3[q - 2][1, 0]
            for d in range(1, NZ):
                total = total + recv3[q - 2][v, d]
            finish(v, q, total)

    sum_rows(0)
    link(0, 2)
    link(0, 3)
    sum_rows(1)
    link(0, 4)
    link(1, 2)
    middle(0)
    sum_rows(2)
    link(1, 3)
    sum_rows(3)
    s_middle(2)
    link(1, 4)
    s_middle(3)
    middle(1)
    last_y(0)
    s_last(2)
    s_last(3)
    last_y(1)

    for v in range(2):
        for q in range(CHUNKS):
            for d in range(1, 8):
                row_wait(v, q, d).wait_send()
        for q in range(2):
            for way in range(2):
                for k in range(hops(v, way)):
                    link_copy(v, q, way, k + 1).wait_send()
            for d in range(1, 4):
                y_copy(v, q, d).wait_send()
                s2_copy(v, q + 2, d).wait_send()
            for d in range(1, NZ):
                s3_copy(v, q + 2, d).wait_send()

    @pl.when(x != y)
    def _():
        for q in range(2):
            y_copy(1, q, 0).wait_send()
            s3_copy(1, q + 2, 0).wait_send()


def shards(wavefunction, left_blocks, right_blocks, target_owner, target_local):
    o, s = lax.axis_index("ops"), lax.axis_index("sec")
    owner = lax.dynamic_index_in_dim(target_owner[0, :, :, :, 0], s, 0, keepdims=False)
    local = lax.dynamic_index_in_dim(target_local[0], s, 0, keepdims=False)
    number = owner % NY * (NZ * SECTORS) + owner // NY * SECTORS + local
    line = number.T.reshape(1, PAIRS)
    lanes = jnp.arange(128, dtype=jnp.int32)[None, :]
    table = jnp.where(lanes // PAIRS == o % 2, jnp.concatenate([line, line], axis=1), 0)
    table = jnp.broadcast_to(table, (8, 128))
    far = pl.BlockSpec(memory_space=pltpu.HBM)
    near = pl.BlockSpec(memory_space=pltpu.VMEM)
    dma = pltpu.SemaphoreType.DMA

    def vmem(*shape):
        return pltpu.VMEM(shape, F32)

    return pl.pallas_call(
        kernel,
        out_shape=jax.ShapeDtypeStruct((SECTORS, 2, 16, STATES), F32),
        in_specs=[near, far, far, far],
        out_specs=near,
        scratch_shapes=[
            vmem(SECTORS, 2, STATES, STATES),
            vmem(SECTORS, TERMS, STATES, STATES),
            vmem(SECTORS, TERMS, STATES, STATES),
            pltpu.VMEM((2, 8, 8, 128), jnp.int32),
            pltpu.VMEM((2, TARGETS, 512), BF16),
            *[vmem(2, 8, SECTORS, n * TERMS, 128) for n in ROWS],
            *[vmem(2, 8, SECTORS, n * TERMS, 128) for n in ROWS],
            *[vmem(2, 4, NZ, n * SECTORS, 128) for n in ROWS],
            *[vmem(2, 2, 4, 4, n * SECTORS, 128) for n in ROWS[:2]],
            *[vmem(2, 4, n * SECTORS, 128) for n in ROWS[:2]],
            *[vmem(2, 4, n * SECTORS, 128) for n in ROWS[:2]],
            *[vmem(2, 4, NZ, n * SECTORS, 128) for n in ROWS[2:]],
            *[vmem(2, NZ, n * SECTORS, 128) for n in ROWS[2:]],
            *[vmem(2, NZ, n * SECTORS, 128) for n in ROWS[2:]],
            dma((3, SECTORS)), dma((2, 8)), dma((2, 8)),
            dma((2, CHUNKS, 8)), dma((2, CHUNKS, 8)), dma((2, CHUNKS)),
            dma((2, 2, 2, 4)), dma((2, 2, 2, 4)),
            dma((2, 2, 4)), dma((2, 2, 4)), dma((2, 2, 4)), dma((2, 2, 4)),
            dma((2, 2, NZ)), dma((2, 2, NZ)),
        ],
        compiler_params=pltpu.CompilerParams(
            collective_id=0, has_side_effects=True, vmem_limit_bytes=62 << 20),
        name="sigma",
    )(table, wavefunction, left_blocks, right_blocks)


def solution(mesh):
    placed = (
        P("sec", None, None, None),
        P("ops", "sec", None, None),
        P("ops", "sec", None, None),
        P("ops", None, None, None, None),
        P("ops", None, None, None),
    )
    return jax.shard_map(
        shards, mesh=mesh, in_specs=placed, out_specs=P("sec", None, "ops", None), check_vma=False
    )
```

time: 101 us -> 92.3 us (0.914); the launches traced: 99 us -> 91.3 us
  Pallas kernels: 94.9 us -> 86.9 us
    pallas_call x1, Pallas kernels: 94.9 us -> 86.9 us  [shards(): pl.pallas_call(kernel, out_shape=jax.ShapeDtypeStruct((SECTORS, 2, 16, ST...]
    unnamed x7 -> x5, local copies, waits for them, and re-layouts: 2.88 us -> 2.56 us
where the time goes in v4:
time: 92.3 us; the launch traced here: 91.3 us
  Pallas kernels  86.9 us (94%)
  local copies, waits for them, and re-layouts  4.28 us (5%)
    pallas_call x1, Pallas kernels, shards(): pl.pallas_call(kernel, out_shape=jax.ShapeDtypeStruct((SECTORS, 2, 16, ST...  86.9 us
    unnamed x5, local copies, waits for them, and re-layouts  2.56 us

profile of v4, /device:TPU:5, one launch (start us, length us, event | category | flops | bytes accessed | tf_op | source)
XLA Modules:
  0.0 91.3 jit_solution(8140402981751715568)
XLA Ops:
  0.0 0.0 copy-start
  0.0 0.8 copy-done
  0.8 0.1 constant_dynamic-slice_fusion.1
  0.9 0.1 copy.9
  1.0 0.8 constant_dynamic-slice_fusion
  1.9 0.1 copy.10
  2.0 0.1 copy.8
  2.1 0.1 concatenate.10
  2.1 0.1 compare_select_fusion
  2.2 0.6 broadcast_in_dim.4.tab_ref
  2.8 86.9 %sigma.1 = f32[8,2,16,128]{3,2,1,0:T(8,128)} custom-call(s32[8,128]{1,0:T(8,128)} %broadcast_in_dim.4.tab_ref, f32[8,2,128,128]{3,2,1,0:T(8,128)} %psi_hbm.1, f32[8,8,128,128]{3,2,1,0:T(8,128)} %left_hbm.1, f32[8,8,128,128]{3,2,1,0:T(8,128)} %right_hbm.1), custom_call_target="tpu_custom_call" | custom-call | tf_op jit(solution)/shard_map/sigma/pallas_call | solution.py:364
  89.8 1.6 %copy.12 = f32[8,2,16,128]{3,2,1,0:T(8,128)} copy(f32[8,2,16,128]{3,2,1,0:T(8,128)} %sigma.1) | data formatting | bytes 262144
  (1 shorter events, 0.0 us)
Async XLA Ops:
  0.0 0.8 copy-start

commit v5 on v4

--- a/solution.py
+++ b/solution.py
@@ -34,8 +34,9 @@
     chain = take(2)
     sendy, recvy = take(2), take(2)
     recv2, sendz, recv3 = take(2), take(2), take(2)
+    sendt, recvt = take(2)
     (in_sem, tab_s, tab_r, s1_s, s1_r, own_sem, l_s, l_r,
-     y_s, y_r, s2_s, s2_r, s3_s, s3_r) = take(14)
+     y_s, y_r, s2_s, s2_r, s3_s, s3_r, t_s, t_r) = take(16)
     o, s = lax.axis_index("ops"), lax.axis_index("sec")
     x, c, y, z = o // 2, o % 2, s % NY, s // NY
     own = (o, y * 2 + c)
@@ -151,7 +152,10 @@
     def s3_copy(v, q, d):
         b = (z + d) % NZ
         return remote(sendz[q - 2].at[v, b], recv3[q - 2].at[v, d],
-                      s3_s.at[q - 2, v, d], s3_r.at[q - 2, v, d], home_peer(v, b))
+                      s3_s.at[q - 2, v, d], s3_r.at[q - 2, v, d], home_peer(v * (q - 2), b))
+
+    def flip_copy():
+        return remote(sendt, recvt, t_s, t_r, dev(y, c, x, z))
 
     def compute(g):
         for i in range(PER):
@@ -283,7 +287,7 @@
                 recv2[q - 2][v, 2] + recv2[q - 2][v, 3])
             for d in range(1, NZ):
                 s3_copy(v, q, d).start()
-            if v == 1:
+            if v == 1 and q == 3:
                 @pl.when(x != y)
                 def _():
                     s3_copy(1, q, 0).start()
@@ -293,17 +297,36 @@
                     recv3[q - 2][1, 0] = sendz[q - 2][1, z]
 
     def s_last(q):
-        for v in range(2):
+        for v in (1, 0):
             for d in range(1, NZ):
                 s3_copy(v, q, d).wait_recv()
-            if v == 1:
+            straight = v == 0 or q == 2
+            if not straight:
                 @pl.when(x != y)
                 def _():
                     s3_copy(1, q, 0).wait_recv()
-            total = sendz[q - 2][0, z] if v == 0 else recv3[q - 2][1, 0]
+            total = sendz[q - 2][v, z] if straight else recv3[q - 2][1, 0]
             for d in range(1, NZ):
                 total = total + recv3[q - 2][v, d]
-            finish(v, q, total)
+            if v == 0 or q == 3:
+                finish(v, q, total)
+            else:
+                sendt[...] = total
+
+                @pl.when(x != y)
+                def _():
+                    flip_copy().start()
+
+                @pl.when(x == y)
+                def _():
+                    recvt[...] = total
+
+    def flip_last():
+        @pl.when(x != y)
+        def _():
+            flip_copy().wait_recv()
+
+        finish(1, 2, recvt[...])
 
     sum_rows(0)
     link(0, 2)
@@ -323,6 +346,7 @@
     s_last(2)
     s_last(3)
     last_y(1)
+    flip_last()
 
     for v in range(2):
         for q in range(CHUNKS):
@@ -342,7 +366,8 @@
     def _():
         for q in range(2):
             y_copy(1, q, 0).wait_send()
-            s3_copy(1, q + 2, 0).wait_send()
+        s3_copy(1, 3, 0).wait_send()
+        flip_copy().wait_send()
 
 
 def shards(wavefunction, left_blocks, right_blocks, target_owner, target_local):
@@ -381,11 +406,13 @@
             *[vmem(2, 4, NZ, n * SECTORS, 128) for n in ROWS[2:]],
             *[vmem(2, NZ, n * SECTORS, 128) for n in ROWS[2:]],
             *[vmem(2, NZ, n * SECTORS, 128) for n in ROWS[2:]],
+            vmem(ROWS[2] * SECTORS, 128),
+            vmem(ROWS[2] * SECTORS, 128),
             dma((3, SECTORS)), dma((2, 8)), dma((2, 8)),
             dma((2, CHUNKS, 8)), dma((2, CHUNKS, 8)), dma((2, CHUNKS)),
             dma((2, 2, 2, 4)), dma((2, 2, 2, 4)),
             dma((2, 2, 4)), dma((2, 2, 4)), dma((2, 2, 4)), dma((2, 2, 4)),
-            dma((2, 2, NZ)), dma((2, 2, NZ)),
+            dma((2, 2, NZ)), dma((2, 2, NZ)), dma, dma,
         ],
         compiler_params=pltpu.CompilerParams(
             collective_id=0, has_side_effects=True, vmem_limit_bytes=62 << 20),

time: 92.3 us -> 89.4 us (0.969)
  Pallas kernels: 86.9 us -> 84.8 us
    pallas_call x1, Pallas kernels: 86.9 us -> 84.8 us  [shards(): pl.pallas_call(kernel, out_shape=jax.ShapeDtypeStruct((SECTORS, 2, 16, ST...]
where the time goes in v5:
time: 89.4 us; the launch traced here: 89.2 us
  Pallas kernels  84.8 us (95%)
  local copies, waits for them, and re-layouts  4.28 us (5%)
    pallas_call x1, Pallas kernels, shards(): pl.pallas_call(kernel, out_shape=jax.ShapeDtypeStruct((SECTORS, 2, 16, ST...  84.8 us
    unnamed x5, local copies, waits for them, and re-layouts  2.56 us

profile of v5, /device:TPU:5, one launch (start us, length us, event | category | flops | bytes accessed | tf_op | source)
XLA Modules:
  0.0 89.2 jit_solution(14339933575414594555)
XLA Ops:
  0.0 0.0 copy-start
  0.0 0.8 copy-done
  0.8 0.1 constant_dynamic-slice_fusion.1
  0.9 0.1 copy.9
  1.0 0.8 constant_dynamic-slice_fusion
  1.9 0.1 copy.10
  2.0 0.1 copy.8
  2.1 0.1 concatenate.10
  2.1 0.1 compare_select_fusion
  2.2 0.6 broadcast_in_dim.4.tab_ref
  2.8 84.8 %sigma.1 = f32[8,2,16,128]{3,2,1,0:T(8,128)} custom-call(s32[8,128]{1,0:T(8,128)} %broadcast_in_dim.4.tab_ref, f32[8,2,128,128]{3,2,1,0:T(8,128)} %psi_hbm.1, f32[8,8,128,128]{3,2,1,0:T(8,128)} %left_hbm.1, f32[8,8,128,128]{3,2,1,0:T(8,128)} %right_hbm.1), custom_call_target="tpu_custom_call" | custom-call | tf_op jit(solution)/shard_map/sigma/pallas_call | solution.py:389
  87.6 1.6 %copy.12 = f32[8,2,16,128]{3,2,1,0:T(8,128)} copy(f32[8,2,16,128]{3,2,1,0:T(8,128)} %sigma.1) | data formatting | bytes 262144
  (1 shorter events, 0.0 us)
Async XLA Ops:
  0.0 0.8 copy-start

commit v6 on v5

--- a/solution.py
+++ b/solution.py
@@ -338,8 +338,8 @@
     sum_rows(2)
     link(1, 3)
     sum_rows(3)
+    link(1, 4)
     s_middle(2)
-    link(1, 4)
     s_middle(3)
     middle(1)
     last_y(0)

time: 89.4 us -> 88.8 us (level); the launches traced: 89.2 us -> 87.6 us
  Pallas kernels: 84.8 us -> 83.2 us
    pallas_call x1, Pallas kernels: 84.8 us -> 83.2 us  [shards(): pl.pallas_call(kernel, out_shape=jax.ShapeDtypeStruct((SECTORS, 2, 16, ST...]
where the time goes in v6:
time: 88.8 us; the launch traced here: 87.6 us
  Pallas kernels  83.2 us (94%)
  local copies, waits for them, and re-layouts  4.28 us (5%)
    pallas_call x1, Pallas kernels, shards(): pl.pallas_call(kernel, out_shape=jax.ShapeDtypeStruct((SECTORS, 2, 16, ST...  83.2 us
    unnamed x5, local copies, waits for them, and re-layouts  2.56 us

profile of v6, /device:TPU:5, one launch (start us, length us, event | category | flops | bytes accessed | tf_op | source)
XLA Modules:
  0.0 87.6 jit_solution(3410950241115058408)
XLA Ops:
  0.0 0.0 copy-start
  0.0 0.8 copy-done
  0.8 0.1 constant_dynamic-slice_fusion.1
  0.9 0.1 copy.9
  1.0 0.8 constant_dynamic-slice_fusion
  1.9 0.1 copy.10
  2.0 0.1 copy.8
  2.1 0.1 concatenate.10
  2.1 0.1 compare_select_fusion
  2.2 0.6 broadcast_in_dim.4.tab_ref
  2.8 83.2 %sigma.1 = f32[8,2,16,128]{3,2,1,0:T(8,128)} custom-call(s32[8,128]{1,0:T(8,128)} %broadcast_in_dim.4.tab_ref, f32[8,2,128,128]{3,2,1,0:T(8,128)} %psi_hbm.1, f32[8,8,128,128]{3,2,1,0:T(8,128)} %left_hbm.1, f32[8,8,128,128]{3,2,1,0:T(8,128)} %right_hbm.1), custom_call_target="tpu_custom_call" | custom-call | tf_op jit(solution)/shard_map/sigma/pallas_call | solution.py:389
  86.0 1.6 %copy.12 = f32[8,2,16,128]{3,2,1,0:T(8,128)} copy(f32[8,2,16,128]{3,2,1,0:T(8,128)} %sigma.1) | data formatting | bytes 262144
  (1 shorter events, 0.0 us)
Async XLA Ops:
  0.0 0.8 copy-start
